TPU v7x, 32 devices: a whole 2x2x4 slice. The times are simulated.
32 devices in a mesh: gx: 4 (over y, x), gy: 8 (over z, core).
Axes of the slice: x: 2, y: 2, z: 4, core: 2. Of those that a mesh axis runs over, the one named last changes fastest.
Arguments:
- tokens: bfloat16 [512, 16384], P(None, ('gx', 'gy')), may hold values from -6 to 6
- gate_weight: bfloat16 [16384, 26624], P('gx', 'gy'), may hold values from -0.046875 to 0.046875
- up_weight: bfloat16 [16384, 26624], P('gx', 'gy'), may hold values from -0.046875 to 0.046875
- down_weight: bfloat16 [26624, 16384], P('gy', 'gx'), may hold values from -0.0390625 to 0.0390625
- mixing: float32 [52, 52], replicated, may hold values from -0.3 to 1.2
Outputs:
- mixed: bfloat16 [512, 16384], P(None, ('gx', 'gy'))
All inputs are finite; a program needn't handle non-finite values.
Results may differ from a plain program's by a relative error of at most 0.025.
Values may be sent and summed in bfloat16 or wider, within the bound.
A program may use at most 192 MiB of HBM per device.

v0:
```python
import jax
import jax.numpy as jnp
from jax import lax
from jax.sharding import PartitionSpec as P


def parity_sign(values):
    ones_count = jnp.zeros_like(values)
    for bit_place in range(20):
        ones_count = ones_count + jnp.bitwise_and(jnp.right_shift(values, bit_place), 1)
    return (1 - 2 * jnp.bitwise_and(ones_count, 1)).astype(jnp.float32)


def sylvester(matrix_order):
    indices = jnp.arange(matrix_order, dtype=jnp.int32)
    common = jnp.bitwise_and(indices[:, None], indices[None, :])
    return parity_sign(common)


def mix_across(hidden):
    position = lax.axis_index("gy")
    segment = lax.all_gather(hidden[None], "gy", axis=0, tiled=True)
    indices = jnp.arange(segment.shape[0], dtype=jnp.int32)
    common = jnp.bitwise_and(indices, position)
    sign_row = parity_sign(common)
    return jnp.tensordot(sign_row, segment.astype(jnp.float32), axes=1)


def on_device(tokens, gate_weight, up_weight, down_weight, mixing):
    col_block = gate_weight.shape[1]
    a_points = mixing.shape[0]
    inner_size = col_block // a_points
    factor = 1.0 / jnp.sqrt(jnp.float32(inner_size * lax.axis_size("gy")))
    highest = lax.Precision.HIGHEST
    segment = lax.all_gather(tokens, "gy", axis=1, tiled=True)
    partial_value = jnp.stack(
        [
            jnp.dot(segment, gate_weight, preferred_element_type=jnp.float32),
            jnp.dot(segment, up_weight, preferred_element_type=jnp.float32),
        ],
        axis=1,
    )
    summed = lax.psum_scatter(partial_value, "gx", scatter_dimension=0, tiled=True)
    hidden = (jax.nn.silu(summed[:, 0]) * summed[:, 1]).astype(jnp.bfloat16)
    blended = mix_across(hidden)
    row_count = blended.shape[0]
    section_one = jnp.einsum(
        "tba,ad->tbd", blended.reshape(row_count, inner_size, a_points), mixing, precision=highest
    )
    section_two = jnp.einsum("tbd,bc->tcd", section_one, sylvester(inner_size), precision=highest)
    rotated = (section_two * factor).astype(jnp.bfloat16).reshape(row_count, col_block)
    all_rows = lax.all_gather(rotated, "gx", axis=0, tiled=True)
    products = jnp.dot(all_rows, down_weight, preferred_element_type=jnp.float32)
    return lax.psum_scatter(products.astype(jnp.bfloat16), "gy", scatter_dimension=1, tiled=True)


def solution(mesh):
    placed = (P(None, ("gx", "gy")), P("gx", "gy"), P("gx", "gy"), P("gy", "gx"), P())
    return jax.shard_map(
        on_device, mesh=mesh, in_specs=placed, out_specs=P(None, ("gx", "gy")), check_vma=False
    )
```

profile of v0, /device:TPU:0, one launch (start us, length us, event | category | flops | bytes accessed | tf_op | source)
XLA Modules:
  0.0 461.7 jit_solution(8941715812542117240)
XLA Ops:
  6.5 0.0 copy-start
  6.5 0.0 all-gather.4.cloned.1.call-start
  6.5 0.7 all-gather.4.cloned.1.call-update
  7.3 0.0 reduce-scatter.3.cloned.1.call-start
  7.3 51.3 %all-gather.4.cloned.1.call-done = bf16[512,4096]{1,0:T(8,128)(2,1)} async-done(((bf16[512,512]{1,0:T(8,128)(2,1)}), bf16[512,4096]{1,0:T(8,128)(2,1)}) %all-gather.4.cloned.1.call-update) | async-done | bytes 4194320 | tf_op jit(solution)/shard_map/all_gather | solution.py:35
  58.6 0.0 copy-start.1
  58.6 27.3 %convolution_bitcast_fusion = f32[512,1,3328]{2,0,1:T(8,128)} fusion(bf16[512,4096]{1,0:T(8,128)(2,1)} %all-gather.4.cloned.1.call-done, bf16[4096,3328]{1,0:T(8,128)(2,1)} %param.7), kind=kOutput, calls=%fused_computation.3 | convolution fusion | flops 13958643712 | bytes 38273024 | tf_op jit(solution)/shard_map/dot_general | solution.py:39
  85.9 0.0 copy-done.1
  85.9 22.3 %convolution_bitcast_fusion.1 = f32[512,1,3328]{2,0,1:T(8,128)} fusion(bf16[512,4096]{1,0:T(8,128)(2,1)S(1)} %copy-done.1, bf16[4096,3328]{1,0:T(8,128)(2,1)} %param.6), kind=kOutput, calls=%fused_computation.4 | convolution fusion | flops 13958643712 | bytes 38273024 | tf_op jit(solution)/shard_map/dot_general | solution.py:38
  108.2 10.7 %pad_maximum_fusion = f32[512,2,3328]{2,0,1:T(8,128)} fusion(f32[512,1,3328]{2,0,1:T(8,128)} %convolution_bitcast_fusion, f32[512,1,3328]{2,0,1:T(8,128)} %convolution_bitcast_fusion.1), kind=kLoop, calls=%fused_computation | loop fusion | flops 3407872 | bytes 27262976 | tf_op jit(solution)/shard_map/stack | solution.py:36
  118.9 0.0 reduce-scatter.3.cloned.1.call-update
  118.9 0.0 all-gather.6.cloned.1.call-start
  118.9 128.1 %reduce-scatter.3.cloned.1.call-done = f32[128,2,3328]{2,0,1:T(8,128)} async-done(((f32[512,2,3328]{2,0,1:T(8,128)}), f32[128,2,3328]{2,0,1:T(8,128)}) %reduce-scatter.3.cloned.1.call-update) | async-done | bytes 3407888 | tf_op jit(solution)/shard_map/reduce_scatter | solution.py:43
  247.0 3.3 fusion.3
  250.4 0.0 all-gather.6.cloned.1.call-update
  250.4 0.0 all-gather.8.cloned.1.call-start
  250.4 69.1 %all-gather.6.cloned.1.call-done = bf16[8,128,3328]{2,1,0:T(8,128)(2,1)} async-done(((bf16[1,128,3328]{2,1,0:T(8,128)(2,1)}), bf16[8,128,3328]{2,1,0:T(8,128)(2,1)}) %all-gather.6.cloned.1.call-update) | async-done | bytes 6815760 | tf_op jit(solution)/shard_map/all_gather | solution.py:22
  319.5 9.0 %fusion = f32[1,128,3328]{2,0,1:T(1,128)S(1)} fusion(bf16[8,128,3328]{2,1,0:T(8,128)(2,1)} %all-gather.6.cloned.1.call-done, s32[]{:T(128)S(6)} %axis_index.12), kind=kOutput, calls=%fused_computation.1 | convolution fusion | flops 6816256 | bytes 8519684 | tf_op jit(solution)/shard_map/dot_general | solution.py:26
  328.6 3.3 copy.11
  331.9 1.5 reshape.47
  333.3 0.0 copy-done
  333.3 1.7 fusion.78
  335.1 1.8 fusion.8
  336.8 0.6 copy.9
  337.4 1.1 reshape.48
  338.5 0.0 all-gather.8.cloned.1.call-update
  338.5 0.0 reduce-scatter.5.cloned.1.call-start
  338.6 44.6 %all-gather.8.cloned.1.call-done = bf16[512,3328]{0,1:T(8,128)(2,1)} async-done(((bf16[128,3328]{0,1:T(8,128)(2,1)}), bf16[512,3328]{0,1:T(8,128)(2,1)}) %all-gather.8.cloned.1.call-update) | async-done | bytes 3407888 | tf_op jit(solution)/shard_map/all_gather | solution.py:52
  383.2 21.9 %convolution_convert_fusion = bf16[512,4096]{1,0:T(8,128)(2,1)} fusion(bf16[512,3328]{0,1:T(8,128)(2,1)} %all-gather.8.cloned.1.call-done, bf16[3328,4096]{1,0:T(8,128)(2,1)} %param.8), kind=kOutput, calls=%fused_computation.5 | convolution fusion | flops 13960740864 | bytes 34865152 | tf_op jit(solution)/shard_map/dot_general | solution.py:53
  405.0 0.0 reduce-scatter.5.cloned.1.call-update
  405.1 50.1 %reduce-scatter.5.cloned.1.call-done = bf16[512,512]{1,0:T(8,128)(2,1)} async-done(((bf16[512,4096]{1,0:T(8,128)(2,1)}), bf16[512,512]{1,0:T(8,128)(2,1)}) %reduce-scatter.5.cloned.1.call-update) | async-done | bytes 524304 | tf_op jit(solution)/shard_map/reduce_scatter | solution.py:54
Async XLA Ops:
  6.5 326.8 %copy-start = (f32[52,52]{1,0:T(8,128)S(1)}, f32[52,52]{1,0:T(8,128)}, u32[]{:S(2)}) copy-start(f32[52,52]{1,0:T(8,128)} %param.9) | copy-start | bytes 32452
  6.5 52.0 %all-gather.4.cloned.1.call-start = ((), (), s32[]{:S(2)}) async-start(), calls=%async_computation.2 | async-start | bytes 4718592 | tf_op jit(solution)/shard_map/all_gather | solution.py:35
  7.3 239.8 %reduce-scatter.3.cloned.1.call-start = ((), (), s32[]{:S(2)}) async-start(), calls=%async_computation.3 | async-start | bytes 17039360 | tf_op jit(solution)/shard_map/reduce_scatter | solution.py:43
  58.6 27.3 %copy-start.1 = (bf16[512,4096]{1,0:T(8,128)(2,1)S(1)}, bf16[512,4096]{1,0:T(8,128)(2,1)}, u32[]{:S(2)}) copy-start(bf16[512,4096]{1,0:T(8,128)(2,1)} %all-gather.4.cloned.1.call-done) | copy-start | bytes 12582916
  118.9 200.7 %all-gather.6.cloned.1.call-start = ((), (), s32[]{:S(2)}) async-start(), calls=%async_computation.4 | async-start | bytes 7667712 | tf_op jit(solution)/shard_map/all_gather | solution.py:22
  250.4 132.8 %all-gather.8.cloned.1.call-start = ((), (), s32[]{:S(2)}) async-start(), calls=%async_computation.5 | async-start | bytes 4259840 | tf_op jit(solution)/shard_map/all_gather | solution.py:52
  338.5 116.6 %reduce-scatter.5.cloned.1.call-start = ((), (), s32[]{:S(2)}) async-start(), calls=%async_computation.6 | async-start | bytes 4718592 | tf_op jit(solution)/shard_map/reduce_scatter | solution.py:54
Sparse Core Ops, SparseCore 0:
  8.9 49.5 all-gather.3
  119.0 127.9 reduce-scatter.2
  250.5 69.0 all-gather.5
  338.6 44.4 all-gather.7
  405.2 49.8 reduce-scatter.4
where the time goes:
time: 462 us
  waiting for transfers between devices  344 us (74%)
  matrix products  84 us (18%)
  other arithmetic  14 us (3%)
  between operations  13.2 us (3%)
  local copies, waits for them, and re-layouts  6.42 us (1%)
    reduce_scatter x1, waiting for transfers between devices, on_device(): lax.psum_scatter(partial_value, 'gx', scatter_dimension=0, tiled=True)  128 us
    all_gather x1, waiting for transfers between devices, mix_across(): segment = lax.all_gather(hidden[None], 'gy', axis=0, tiled=True)  69.1 us
    all_gather x1, waiting for transfers between devices, on_device(): segment = lax.all_gather(tokens, 'gy', axis=1, tiled=True)  51.3 us
    reduce_scatter x1, waiting for transfers between devices, on_device(): lax.psum_scatter(products.astype(jnp.bfloat16), 'gy', scatter_dimension=1...  50.1 us
    all_gather x1, waiting for transfers between devices, on_device(): all_rows = lax.all_gather(rotated, 'gx', axis=0, tiled=True)  44.6 us
    dot_general x1, matrix products, on_device(): jnp.dot(segment, up_weight, preferred_element_type=jnp.float32)  27.3 us
    dot_general x1, matrix products, on_device(): jnp.dot(segment, gate_weight, preferred_element_type=jnp.float32)  22.3 us
    dot_general x1, matrix products, on_device(): jnp.dot(all_rows, down_weight, preferred_element_type=jnp.float32)  21.9 us
  transfers between devices with their start and end apart: 5, of which 5 were waited for; matrix products, arithmetic and copies ran while one was open for 0% of the time, Pallas kernels for 0%

commit v1 on v0

--- a/solution.py
+++ b/solution.py
@@ -2,6 +2,17 @@
 import jax.numpy as jnp
 from jax import lax
 from jax.sharding import PartitionSpec as P
+
+
+def gather_by_hops(value, axis, along):
+    peers = lax.axis_size(axis)
+    right = [(i, (i + 1) % peers) for i in range(peers)]
+    blocks = [value]
+    for hop in range(1, peers):
+        blocks = [lax.ppermute(blocks[0], axis, right), *blocks]
+    out = jnp.concatenate(blocks, axis=along)
+    places = (lax.axis_index(axis) + 1) * blocks[-1].shape[along]
+    return jnp.roll(out, places, axis=along)
 
 
 def parity_sign(values):
@@ -49,7 +60,7 @@
     )
     section_two = jnp.einsum("tbd,bc->tcd", section_one, sylvester(inner_size), precision=highest)
     rotated = (section_two * factor).astype(jnp.bfloat16).reshape(row_count, col_block)
-    all_rows = lax.all_gather(rotated, "gx", axis=0, tiled=True)
+    all_rows = gather_by_hops(rotated, "gx", 0)
     products = jnp.dot(all_rows, down_weight, preferred_element_type=jnp.float32)
     return lax.psum_scatter(products.astype(jnp.bfloat16), "gy", scatter_dimension=1, tiled=True)
 

time: 462 us -> 479 us (1.037)
  waiting for transfers between devices: 344 us -> 358 us
    ppermute x0 -> x3, waiting for transfers between devices: none -> 61.3 us  [gather_by_hops(): blocks = [lax.ppermute(blocks[0], axis, right), *blocks]]
    all_gather x1 -> x0, waiting for transfers between devices: 44.6 us -> none  [on_device(): all_rows = lax.all_gather(rotated, 'gx', axis=0, tiled=True)]
  transfers between devices with their start and end apart: 5 -> 7, of which waited for: 5 -> 7; matrix products, arithmetic and copies ran while one was open for 0% -> 0% of each run, Pallas kernels for 0% -> 0%
where the time goes in v1:
time: 479 us
  waiting for transfers between devices  358 us (75%)
  matrix products  83.7 us (17%)
  other arithmetic  14 us (3%)
  between operations  13.2 us (3%)
  local copies, waits for them, and re-layouts  7.79 us (2%)
    reduce_scatter x1, waiting for transfers between devices, on_device(): lax.psum_scatter(partial_value, 'gx', scatter_dimension=0, tiled=True)  128 us
    all_gather x1, waiting for transfers between devices, mix_across(): segment = lax.all_gather(hidden[None], 'gy', axis=0, tiled=True)  69.1 us
    ppermute x3, waiting for transfers between devices, gather_by_hops(): blocks = [lax.ppermute(blocks[0], axis, right), *blocks]  61.3 us
    all_gather x1, waiting for transfers between devices, on_device(): segment = lax.all_gather(tokens, 'gy', axis=1, tiled=True)  51.3 us
    reduce_scatter x1, waiting for transfers between devices, on_device(): lax.psum_scatter(products.astype(jnp.bfloat16), 'gy', scatter_dimension=1...  47.8 us
    dot_general x1, matrix products, on_device(): jnp.dot(segment, up_weight, preferred_element_type=jnp.float32)  27.3 us
    dot_general x1, matrix products, on_device(): jnp.dot(segment, gate_weight, preferred_element_type=jnp.float32)  22.3 us
    dot_general x1, matrix products, on_device(): jnp.dot(all_rows, down_weight, preferred_element_type=jnp.float32)  21.5 us
  transfers between devices with their start and end apart: 7, of which 7 were waited for; matrix products, arithmetic and copies ran while one was open for 0% of the time, Pallas kernels for 0%

profile of v1, /device:TPU:0, one launch (start us, length us, event | category | flops | bytes accessed | tf_op | source)
XLA Modules:
  0.0 479.3 jit_solution(15941951800210032179)
XLA Ops:
  6.5 0.0 copy-start
  6.5 0.0 all-gather.3.cloned.1.call-start
  6.5 0.7 all-gather.3.cloned.1.call-update
  7.3 0.0 reduce-scatter.3.cloned.1.call-start
  7.3 51.3 %all-gather.3.cloned.1.call-done = bf16[512,4096]{1,0:T(8,128)(2,1)} async-done(((bf16[512,512]{1,0:T(8,128)(2,1)}), bf16[512,4096]{1,0:T(8,128)(2,1)}) %all-gather.3.cloned.1.call-update) | async-done | bytes 4194320 | tf_op jit(solution)/shard_map/all_gather | solution.py:46
  58.6 0.0 copy-start.1
  58.6 27.3 %convolution_bitcast_fusion = f32[512,1,3328]{2,0,1:T(8,128)} fusion(bf16[512,4096]{1,0:T(8,128)(2,1)} %all-gather.3.cloned.1.call-done, bf16[4096,3328]{1,0:T(8,128)(2,1)} %param.7), kind=kOutput, calls=%fused_computation.3 | convolution fusion | flops 13958643712 | bytes 38273024 | tf_op jit(solution)/shard_map/dot_general | solution.py:50
  85.9 0.0 copy-done.1
  85.9 22.3 %convolution_bitcast_fusion.1 = f32[512,1,3328]{2,0,1:T(8,128)} fusion(bf16[512,4096]{1,0:T(8,128)(2,1)S(1)} %copy-done.1, bf16[4096,3328]{1,0:T(8,128)(2,1)} %param.6), kind=kOutput, calls=%fused_computation.4 | convolution fusion | flops 13958643712 | bytes 38273024 | tf_op jit(solution)/shard_map/dot_general | solution.py:49
  108.2 10.7 %pad_maximum_fusion = f32[512,2,3328]{2,0,1:T(8,128)} fusion(f32[512,1,3328]{2,0,1:T(8,128)} %convolution_bitcast_fusion, f32[512,1,3328]{2,0,1:T(8,128)} %convolution_bitcast_fusion.1), kind=kLoop, calls=%fused_computation | loop fusion | flops 3407872 | bytes 27262976 | tf_op jit(solution)/shard_map/stack | solution.py:47
  118.9 0.0 reduce-scatter.3.cloned.1.call-update
  118.9 0.0 all-gather.5.cloned.1.call-start
  118.9 128.1 %reduce-scatter.3.cloned.1.call-done = f32[128,2,3328]{2,0,1:T(8,128)} async-done(((f32[512,2,3328]{2,0,1:T(8,128)}), f32[128,2,3328]{2,0,1:T(8,128)}) %reduce-scatter.3.cloned.1.call-update) | async-done | bytes 3407888 | tf_op jit(solution)/shard_map/reduce_scatter | solution.py:54
  247.0 3.3 fusion.4
  250.4 0.0 all-gather.5.cloned.1.call-update
  250.4 0.0 reduce-scatter.5.cloned.1.call-start
  250.4 69.1 %all-gather.5.cloned.1.call-done = bf16[8,128,3328]{2,1,0:T(8,128)(2,1)} async-done(((bf16[1,128,3328]{2,1,0:T(8,128)(2,1)}), bf16[8,128,3328]{2,1,0:T(8,128)(2,1)}) %all-gather.5.cloned.1.call-update) | async-done | bytes 6815760 | tf_op jit(solution)/shard_map/all_gather | solution.py:33
  319.5 9.0 %fusion = f32[1,128,3328]{2,0,1:T(1,128)S(1)} fusion(bf16[8,128,3328]{2,1,0:T(8,128)(2,1)} %all-gather.5.cloned.1.call-done, s32[]{:T(128)S(6)} %axis_index.22), kind=kOutput, calls=%fused_computation.1 | convolution fusion | flops 6816256 | bytes 8519684 | tf_op jit(solution)/shard_map/dot_general | solution.py:37
  328.6 3.3 copy.11
  331.9 1.5 reshape.47
  333.3 0.0 copy-done
  333.3 1.7 fusion.79
  335.1 1.8 fusion.9
  336.8 0.6 copy.9
  337.4 0.2 reshape.48
  337.6 1.5 collective-permute-start
  339.1 20.5 %collective-permute-done = bf16[128,3328]{0,1:T(8,128)(2,1)S(1)} collective-permute-done((bf16[128,3328]{0,1:T(8,128)(2,1)S(1)}, bf16[128,3328]{0,1:T(8,128)(2,1)S(1)}, u32[]{:S(2)}, u32[]{:S(2)}) %collective-permute-start) | collective-permute-done | bytes 852000 | tf_op jit(solution)/shard_map/ppermute | solution.py:12
  359.6 0.6 collective-permute-start.1
  360.2 20.5 %collective-permute-done.1 = bf16[128,3328]{0,1:T(8,128)(2,1)S(1)} collective-permute-done((bf16[128,3328]{0,1:T(8,128)(2,1)S(1)}, bf16[128,3328]{0,1:T(8,128)(2,1)S(1)}, u32[]{:S(2)}, u32[]{:S(2)}) %collective-permute-start.1) | collective-permute-done | bytes 852000 | tf_op jit(solution)/shard_map/ppermute | solution.py:12
  380.7 0.0 collective-permute-start.2
  380.7 20.3 %collective-permute-done.2 = bf16[128,3328]{0,1:T(8,128)(2,1)S(1)} collective-permute-done((bf16[128,3328]{0,1:T(8,128)(2,1)S(1)}, bf16[128,3328]{0,1:T(8,128)(2,1)S(1)}, u32[]{:S(2)}, u32[]{:S(2)}) %collective-permute-start.2) | collective-permute-done | bytes 852000 | tf_op jit(solution)/shard_map/ppermute | solution.py:12
  401.0 0.2 constant_dynamic-update-slice_fusion.7
  401.2 0.3 constant_dynamic-update-slice_fusion.6
  401.5 0.3 constant_dynamic-update-slice_fusion.5
  401.8 0.3 constant_dynamic-update-slice_fusion.4
  402.1 0.3 constant_dynamic-update-slice_fusion.3
  402.4 0.3 constant_dynamic-update-slice_fusion.2
  402.7 0.3 constant_dynamic-update-slice_fusion.1
  403.0 0.3 constant_dynamic-update-slice_fusion
  403.3 21.5 %convolution_convert_fusion = bf16[512,4096]{1,0:T(8,128)(2,1)} fusion(bf16[3328,4096]{1,0:T(8,128)(2,1)} %param.8, bf16[1024,3328]{0,1:T(8,128)(2,1)S(1)} %constant_dynamic-update-slice_fusion, s32[]{:T(128)S(6)} %select_n.14), kind=kOutput, calls=%fused_computation.5 | convolution fusion | flops 13960740864 | bytes 34865156 | tf_op jit(solution)/shard_map/dot_general | solution.py:64
  424.9 0.0 reduce-scatter.5.cloned.1.call-update
  424.9 47.8 %reduce-scatter.5.cloned.1.call-done = bf16[512,512]{1,0:T(8,128)(2,1)} async-done(((bf16[512,4096]{1,0:T(8,128)(2,1)}), bf16[512,512]{1,0:T(8,128)(2,1)}) %reduce-scatter.5.cloned.1.call-update) | async-done | bytes 524304 | tf_op jit(solution)/shard_map/reduce_scatter | solution.py:65
Async XLA Ops:
  6.5 326.8 %copy-start = (f32[52,52]{1,0:T(8,128)S(1)}, f32[52,52]{1,0:T(8,128)}, u32[]{:S(2)}) copy-start(f32[52,52]{1,0:T(8,128)} %param.9) | copy-start | bytes 32452
  6.5 52.0 %all-gather.3.cloned.1.call-start = ((), (), s32[]{:S(2)}) async-start(), calls=%async_computation.2 | async-start | bytes 4718592 | tf_op jit(solution)/shard_map/all_gather | solution.py:46
  7.3 239.8 %reduce-scatter.3.cloned.1.call-start = ((), (), s32[]{:S(2)}) async-start(), calls=%async_computation.3 | async-start | bytes 17039360 | tf_op jit(solution)/shard_map/reduce_scatter | solution.py:54
  58.6 27.3 %copy-start.1 = (bf16[512,4096]{1,0:T(8,128)(2,1)S(1)}, bf16[512,4096]{1,0:T(8,128)(2,1)}, u32[]{:S(2)}) copy-start(bf16[512,4096]{1,0:T(8,128)(2,1)} %all-gather.3.cloned.1.call-done) | copy-start | bytes 12582916
  118.9 200.7 %all-gather.5.cloned.1.call-start = ((), (), s32[]{:S(2)}) async-start(), calls=%async_computation.4 | async-start | bytes 7667712 | tf_op jit(solution)/shard_map/all_gather | solution.py:33
  250.4 222.3 %reduce-scatter.5.cloned.1.call-start = ((), (), s32[]{:S(2)}) async-start(), calls=%async_computation.5 | async-start | bytes 4718592 | tf_op jit(solution)/shard_map/reduce_scatter | solution.py:65
  337.6 22.0 %collective-permute-start = (bf16[128,3328]{0,1:T(8,128)(2,1)S(1)}, bf16[128,3328]{0,1:T(8,128)(2,1)S(1)}, u32[]{:S(2)}, u32[]{:S(2)}) collective-permute-start(bf16[128,3328]{0,1:T(8,128)(2,1)S(1)} %reshape.48), channel_id=1, source_target_pairs={{0,8},{8,16},{16,24},{24,0},{1,9},{9,17},{17,25},{25,1},{2,10},{10... | collective-permute-start | bytes 2555912 | tf_op jit(solution)/shard_map/ppermute | solution.py:12
  359.6 21.1 %collective-permute-start.1 = (bf16[128,3328]{0,1:T(8,128)(2,1)S(1)}, bf16[128,3328]{0,1:T(8,128)(2,1)S(1)}, u32[]{:S(2)}, u32[]{:S(2)}) collective-permute-start(bf16[128,3328]{0,1:T(8,128)(2,1)S(1)} %collective-permute-done), channel_id=1, source_target_pairs={{0,8},{8,16},{16,24},{24,0},{1,9},{9,17},{17,25},{25,1},{2,10},{10... | collective-permute-start | bytes 2555912 | tf_op jit(solution)/shard_map/ppermute | solution.py:12
  380.7 20.3 %collective-permute-start.2 = (bf16[128,3328]{0,1:T(8,128)(2,1)S(1)}, bf16[128,3328]{0,1:T(8,128)(2,1)S(1)}, u32[]{:S(2)}, u32[]{:S(2)}) collective-permute-start(bf16[128,3328]{0,1:T(8,128)(2,1)S(1)} %collective-permute-done.1), channel_id=1, source_target_pairs={{0,8},{8,16},{16,24},{24,0},{1,9},{9,17},{17,25},{25,1},{2,10},{10... | collective-permute-start | bytes 2555912 | tf_op jit(solution)/shard_map/ppermute | solution.py:12
Sparse Core Ops, SparseCore 0:
  8.9 49.5 all-gather.2
  119.0 127.9 reduce-scatter.2
  250.5 69.0 all-gather.4
  425.0 47.6 reduce-scatter.4
